TPU v7x, 256 devices: a whole 4x4x8 slice. The times are simulated.
256 devices in a mesh: row: 32 (over y, z), col: 8 (over x, core).
Axes of the slice: x: 4, y: 4, z: 8, core: 2. Of those that a mesh axis runs over, the one named last changes fastest.
Arguments:
- load_currents: float32 [16, 256, 128, 128], P(None, 'row', 'col'), may hold values from -24 to 24
- block_library: float32 [8, 128, 128], replicated, may hold values from -4.0625 to 24.1, as said below
- strap_conductance: float32 [2, 128], replicated, may hold values from 0.5 to 4
- block_types: int32 [256, 128], P('row', 'col'), may hold values from 0 to 7
- aggregate_map: int32 [256, 128], P('row', 'col'), may hold values from 0 to 255, as said below
Outputs:
- node_voltage: float32 [16, 256, 128, 128], P(None, 'row', 'col')
- residual: float32 [16, 256, 128, 128], P(None, 'row', 'col')
Inputs may be any that keep to these rules, and one draw needn't show every extreme that they name: `aggregate_map`: each aggregate id names an aggregate of one column group of 16 block columns; the same id in another column group is another aggregate. Every aggregate of every column group holds at least one block. `block_library`: each library block is symmetric positive definite, with nonpositive off-diagonal entries and positive row sums.
All inputs are finite; a program needn't handle non-finite values.
Results may differ from a plain program's by a relative error of at most 0.0003.
Values sent between devices are 32-bit elements; how exact they have to be, the bound alone decides.
A program may use at most 64 MiB of HBM per device.

v0:
```python
import jax
import jax.numpy as jnp
from jax import lax
from jax.sharding import PartitionSpec as P

SWEEPS = 3
ITERS = 2
AGR = 4
AGC = 4


def padded_2(array, sides, width):
    for axis, dim in sides:
        size, length = (lax.axis_size(axis), array.shape[dim])
        up = [(i, (i + 1) % size) for i in range(size - 1)]
        down = [(j, i) for i, j in up]
        last = lax.slice_in_dim(array, length - width, length, axis=dim)
        first = lax.slice_in_dim(array, 0, width, axis=dim)
        before = lax.ppermute(last, axis, up)
        after = lax.ppermute(first, axis, down)
        array = jnp.concatenate([before, array, after], axis=dim)
    return array


def from_behind(array, axis, by):
    length = lax.axis_size(axis)
    pairs = [(i, i + by) for i in range(length) if 0 <= i + by < length]
    return lax.ppermute(array, axis, pairs)


def coarse_terms(group_ids, group_types, block_sums, north_weight, east_weight, count):
    centre = block_sums[group_types] + 2.0 * north_weight + 2.0 * east_weight
    flat = group_ids.reshape(-1)
    upper = group_ids[:-1].reshape(-1)
    lower = group_ids[1:].reshape(-1)
    left = group_ids[:, :-1].reshape(-1)
    right = group_ids[:, 1:].reshape(-1)
    index = jnp.concatenate(
        [
            flat * count + flat,
            upper * count + lower,
            lower * count + upper,
            left * count + right,
            right * count + left,
        ]
    )
    values = jnp.concatenate(
        [
            centre.reshape(-1),
            -north_weight * jnp.ones((2 * upper.shape[0],), jnp.float32),
            -east_weight * jnp.ones((2 * left.shape[0],), jnp.float32),
        ]
    )
    return jax.ops.segment_sum(values, index, num_segments=count * count).reshape(count, count)


def alignment_sum(residual, zeta):
    return lax.psum(jnp.sum(residual * zeta, axis=(1, 2, 3)), ("row", "col"))


def on_device(load_currents, block_library, strap_conductance, block_types, aggregate_map):
    sizings, rows_local, cols_local, nodes = load_currents.shape
    blocks = rows_local * cols_local
    count = rows_local * lax.axis_size("row") // AGR * (cols_local // AGC)
    picked = block_library[block_types.reshape(-1)]
    couple = 2.0 * strap_conductance[0] + 2.0 * strap_conductance[1]
    diag_library = jnp.diagonal(block_library, axis1=1, axis2=2)
    diagonal = diag_library[block_types] + couple
    block_sums = jnp.sum(block_library, axis=(1, 2))
    north_weight = jnp.sum(strap_conductance[0])
    east_weight = jnp.sum(strap_conductance[1])

    def block_products(field):
        flat = field.reshape(sizings, blocks, nodes)
        product = jnp.einsum("bij,sbj->sbi", picked, flat, precision=lax.Precision.HIGHEST)
        return product.reshape(sizings, rows_local, cols_local, nodes)

    local_matrix = coarse_terms(
        aggregate_map, block_types, block_sums, north_weight, east_weight, count
    )
    below_ids = from_behind(aggregate_map[0], "row", -1)
    present = (lax.axis_index("row") < lax.axis_size("row") - 1).astype(jnp.float32)
    bottom_ids = aggregate_map[-1]
    cross_index = jnp.concatenate([bottom_ids * count + below_ids, below_ids * count + bottom_ids])
    cross_values = -north_weight * present * jnp.ones((2 * cols_local,), jnp.float32)
    cross_matrix = jax.ops.segment_sum(
        cross_values, cross_index, num_segments=count * count
    ).reshape(count, count)
    coarse_matrix = lax.psum(local_matrix + cross_matrix, "row")
    factor = jnp.linalg.cholesky(coarse_matrix)
    flat_ids = aggregate_map.reshape(-1)

    def smooth(residual):
        result = residual / diagonal
        for sweep in range(SWEEPS - 1):
            image = block_products(result) + couple * result
            result = result + (residual - image) / diagonal
        return result

    def coarse_part(residual):
        sums = residual.sum(-1).reshape(sizings, blocks).T
        local = jax.ops.segment_sum(sums, flat_ids, num_segments=count)
        gathered = lax.psum(local, "row")
        solved = jax.scipy.linalg.cho_solve((factor, True), gathered)
        return solved[flat_ids].T.reshape(sizings, rows_local, cols_local)[..., None]

    def precondition(residual):
        return smooth(residual) + coarse_part(residual)

    node_voltage = jnp.zeros_like(load_currents)
    residual = load_currents
    zeta = precondition(residual)
    direction = zeta
    aligned = alignment_sum(residual, zeta)
    for iteration in range(ITERS):
        padded = padded_2(direction, (("row", 1), ("col", 2)), 1)
        north = padded[:, :-2, 1:-1]
        south = padded[:, 2:, 1:-1]
        west = padded[:, 1:-1, :-2]
        east = padded[:, 1:-1, 2:]
        lateral = strap_conductance[0] * (2.0 * direction - north - south) + strap_conductance[
            1
        ] * (2.0 * direction - west - east)
        image = block_products(direction) + lateral
        curvature = lax.psum(jnp.sum(direction * image, axis=(1, 2, 3)), ("row", "col"))
        step_size = (aligned / curvature)[:, None, None, None]
        node_voltage = node_voltage + step_size * direction
        residual = residual - step_size * image
        if iteration + 1 < ITERS:
            zeta = precondition(residual)
            fresh = alignment_sum(residual, zeta)
            blend = (fresh / aligned)[:, None, None, None]
            direction = zeta + blend * direction
            aligned = fresh
    return (node_voltage, residual)


def solution(mesh):
    placed = (P(None, "row", "col", None), P(), P(), P("row", "col"), P("row", "col"))
    return jax.shard_map(
        on_device,
        mesh=mesh,
        in_specs=placed,
        out_specs=(P(None, "row", "col", None), P(None, "row", "col", None)),
        check_vma=False,
    )
```

profile of v0, /device:TPU:1, one launch (start us, length us, event | category | flops | bytes accessed | tf_op | source)
XLA Modules:
  0.0 772.3 jit_solution(3687097905419126397)
XLA Ops:
  7.2 0.7 slice_bitcast_fusion.10
  8.0 1.3 collective-permute-start
  9.3 1.4 slice_reduce_fusion.1
  13.2 0.8 fusion.48
  14.0 0.8 fusion.49
  14.8 0.8 reshape.186
  15.6 0.8 broadcast_in_dim_reshape.2
  16.3 0.8 add_multiply_fusion
  17.8 0.8 reshape.182
  18.7 5.9 copy.47
  25.0 1.8 gather_fusion
  26.8 1.2 gather_fusion.3
  28.8 4.3 gather_fusion.2
  33.8 16.3 %fusion.50 = f32[128,16,128]{2,1,0:T(8,128)S(1)} fusion(f32[16,128,128]{2,0,1:T(8,128)S(1)} %bitcast.139, f32[128,128,128]{2,1,0:T(8,128)} %gather_fusion.2), kind=kOutput, calls=%fused_computation.144 | convolution fusion | flops 402653184 | bytes 10485760 | tf_op jit(solution)/shard_map/bij,sbj->sbi/dot_general | solution.py:75
  50.8 14.2 %fusion.51 = f32[128,16,128]{2,1,0:T(8,128)} fusion(f32[16,128,128]{2,0,1:T(8,128)S(1)} %bitcast.140, f32[128,128,128]{2,1,0:T(8,128)S(1)} %bitcast.127), kind=kOutput, calls=%fused_computation.145 | convolution fusion | flops 402653184 | bytes 10485760 | tf_op jit(solution)/shard_map/bij,sbj->sbi/dot_general | solution.py:75
  65.3 0.7 fusion.42
  66.2 4.7 scatter_custom_fusion
  71.0 0.8 copy.52
  72.3 1.7 scatter_custom_fusion.1
  74.0 120.6 %psum.50 = f32[256,16]{0,1:T(8,128)S(1)} all-reduce(f32[256,16]{0,1:T(8,128)S(1)} %copy.55), channel_id=1, replica_groups=mesh['row'=32,'col'=8] {'row'}, use_global_device_ids=true, to_apply=%region_11.12 | all-reduce | flops 4096 | bytes 32768 | tf_op jit(solution)/shard_map/psum | solution.py:103
  194.7 23.6 %all-reduce.5.cloned.1.call-done = f32[256,256]{0,1:T(8,128)} async-done(((f32[256,256]{0,1:T(8,128)}), f32[256,256]{0,1:T(8,128)}) %all-reduce.5.cloned.1.call-update) | async-done | bytes 262160 | tf_op jit(solution)/shard_map/psum | solution.py:89
  218.2 1.1 copy.53
  219.3 1.0 fusion.16
  220.3 11.7 %cholesky.50 = f32[128,128]{1,0:T(8,128)S(1)} custom-call(f32[128,128]{1,0:T(8,128)S(1)} %cholesky.118), custom_call_target="Cholesky" | custom-call | tf_op jit(solution)/shard_map/jit(cholesky)/cholesky | solution.py:90
  232.1 9.8 %custom-call.16 = f32[1,128,128]{1,2,0:T(8,128)S(1)} custom-call(f32[1,128,128]{2,1,0:T(8,128)S(1)} %get-tuple-element.55), custom_call_target="InvertDiagBlocksLowerTriangular" | custom-call | tf_op jit(solution)/shard_map/jit(cholesky)/cholesky | solution.py:90
  242.4 11.7 %cholesky.105 = f32[128,128]{1,0:T(8,128)S(1)} custom-call(f32[128,128]{1,0:T(8,128)S(1)} %convolution_subtract_fusion), custom_call_target="Cholesky" | custom-call | tf_op jit(solution)/shard_map/jit(cholesky)/cholesky | solution.py:90
  256.1 3.8 while.4
  256.7 1.3 bitcast_dynamic-update-slice_fusion.2
  258.6 1.3 bitcast_dynamic-update-slice_fusion.2
  260.0 19.8 %custom-call.20 = f32[2,128,128]{1,2,0:T(8,128)S(1)} custom-call(f32[2,128,128]{2,1,0:T(8,128)S(1)} %get-tuple-element.17), custom_call_target="InvertDiagBlocksLowerTriangular" | custom-call | tf_op jit(solution)/shard_map/jit(_cho_solve)/triangular_solve | solution.py:104
  281.8 2.0 add_add_fusion.1
  283.8 1.8 collective-permute-start.1
  285.6 1.3 collective-permute-start.2
  287.6 4.0 collective-permute-done.2
  291.6 9.8 %collective-permute-start.3 = (f32[16,10,1,128]{3,0,2,1:T(8,128)S(1)}, f32[16,10,1,128]{3,0,2,1:T(8,128)S(1)}, u32[]{:S(2)}, u32[]{:S(2)}) collective-permute-start(f32[16,10,1,128]{3,0,2,1:T(8,128)S(1)} %get-tuple-element.44), channel_id=1, source_target_pairs={{0,1},{1,2},{2,3},{3,4},{4,5},{5,6},{6,7},{8,9},{9,10},{10,11},{11... | collective-permute-start | bytes 245768 | tf_op jit(solution)/shard_map/ppermute | solution.py:19
  301.4 1.9 collective-permute-start.4
  303.3 15.4 %fusion.52 = f32[128,16,128]{2,1,0:T(8,128)S(1)} fusion(f32[16,128,128]{2,0,1:T(8,128)S(1)} %bitcast.130, f32[128,128,128]{2,1,0:T(8,128)} %gather_fusion.2), kind=kOutput, calls=%fused_computation.146 | convolution fusion | flops 402653184 | bytes 10485760 | tf_op jit(solution)/shard_map/bij,sbj->sbi/dot_general | solution.py:75
  318.7 1.8 multiply_reduce_fusion.2
  320.5 77.0 %all-reduce.2 = (f32[16]{0:T(128)S(1)}, f32[16]{0:T(128)S(1)}) all-reduce(f32[16]{0:T(128)S(1)} %get-tuple-element.22, f32[16]{0:T(128)S(1)} %get-tuple-element.21), channel_id=1, replica_groups=mesh['row'=32,'col'=8] {'row','col'}, use_global_device_ids=true, to_apply=%region_13.15 | all-reduce | flops 32 | bytes 256 | tf_op jit(solution)/shard_map/psum | solution.py:58
  397.6 2.1 broadcast_divide_fusion
  399.7 15.8 %divide_add_fusion = (f32[16,8,16,128]{3,0,2,1:T(8,128)S(1)}, f32[16,8,16]{0,2,1:T(8,128)S(1)}, f32[128,16,128]{2,1,0:T(8,128)S(1)}) fusion(f32[16,8,16,128]{3,0,2,1:T(8,128)S(1)} %get-tuple-element.38, f32[128]{0:T(128)S(1)} %add_multiply_fusion, f32[8,16,128]{2,1,0:T(8,128)S(1)} %broadcast_add_fusion, f32[16,128,128]{2,0,1:T(8,128)S(1)} %bitcast.137, ...), kind=kOutput, calls=%fused_computation.54 | convolution fusion | flops 404486144 | bytes 12657152 | tf_op jit(solution)/shard_map/bij,sbj->sbi/dot_general | solution.py:75
  415.5 14.0 %fusion.53 = f32[128,16,128]{2,1,0:T(8,128)} fusion(f32[16,128,128]{2,0,1:T(8,128)S(1)} %bitcast.138, f32[128,128,128]{2,1,0:T(8,128)S(1)} %bitcast.129), kind=kOutput, calls=%fused_computation.147 | convolution fusion | flops 402653184 | bytes 10485760 | tf_op jit(solution)/shard_map/bij,sbj->sbi/dot_general | solution.py:75
  429.6 1.9 scatter_custom_fusion.2
  431.5 1.0 copy.61
  432.4 110.4 %psum.53 = f32[256,16]{0,1:T(8,128)S(1)} all-reduce(f32[256,16]{0,1:T(8,128)S(1)} %copy.61), channel_id=1, replica_groups=mesh['row'=32,'col'=8] {'row'}, use_global_device_ids=true, to_apply=%region_18.20 | all-reduce | flops 4096 | bytes 32768 | tf_op jit(solution)/shard_map/psum | solution.py:103
  542.8 1.0 fusion.27
  544.0 1.0 fusion.31
  545.0 1.0 fusion.30
  546.3 1.0 fusion.26
  548.1 1.9 multiply_reduce_fusion.1
  550.0 100.2 %psum.54 = f32[16]{0:T(128)S(1)} all-reduce(f32[16]{0:T(128)S(1)} %multiply_reduce_fusion.1), channel_id=1, replica_groups=mesh['row'=32,'col'=8] {'row','col'}, use_global_device_ids=true, to_apply=%region_20.22 | all-reduce | flops 16 | bytes 128 | tf_op jit(solution)/shard_map/psum | solution.py:58
  650.8 2.1 multiply_add_fusion.1
  652.9 3.7 collective-permute-start.5
  656.6 1.3 collective-permute-start.6
  657.9 0.9 collective-permute-done.5
  658.7 3.6 collective-permute-done.6
  662.3 4.3 collective-permute-start.7
  666.6 1.9 collective-permute-start.8
  668.5 15.4 %fusion.54 = f32[128,16,128]{2,1,0:T(8,128)S(1)} fusion(f32[16,128,128]{2,0,1:T(8,128)S(1)} %bitcast.131, f32[128,128,128]{2,1,0:T(8,128)} %gather_fusion.2), kind=kOutput, calls=%fused_computation.148 | convolution fusion | flops 402653184 | bytes 10485760 | tf_op jit(solution)/shard_map/bij,sbj->sbi/dot_general | solution.py:75
  683.9 1.5 multiply_reduce_fusion
  685.4 75.4 %psum.55 = f32[16]{0:T(128)S(1)} all-reduce(f32[16]{0:T(128)S(1)} %get-tuple-element.35), channel_id=1, replica_groups=mesh['row'=32,'col'=8] {'row','col'}, use_global_device_ids=true, to_apply=%region_22.24 | all-reduce | flops 16 | bytes 128 | tf_op jit(solution)/shard_map/psum | solution.py:125
  760.8 1.6 multiply_subtract_fusion
  762.4 1.3 copy.63
  763.7 1.3 copy.64
  (103 shorter events, 11.3 us)
Async XLA Ops:
  7.2 17.4 %copy-start = (f32[8,128,128]{2,1,0:T(8,128)S(1)}, f32[8,128,128]{2,1,0:T(8,128)}, u32[]{:S(2)}) copy-start(f32[8,128,128]{2,1,0:T(8,128)} %param.8) | copy-start | bytes 1572868
  7.2 211.1 %all-reduce.5.cloned.1.call-start = ((), (), s32[]{:S(2)}) async-start(), calls=%async_computation | async-start | bytes 524288 | tf_op jit(solution)/shard_map/psum | solution.py:89
  8.0 57.3 %collective-permute-start = (s32[16]{0:T(128)S(1)}, s32[16]{0:T(128)S(1)}, u32[]{:S(2)}, u32[]{:S(2)}) collective-permute-start(s32[16]{0:T(128)S(1)} %slice_bitcast_fusion.10), channel_id=1, source_target_pairs={{8,0},{16,8},{24,16},{32,24},{40,32},{48,40},{56,48},{64,56},{72,6... | collective-permute-start | bytes 200 | tf_op jit(solution)/shard_map/ppermute | solution.py:28
  15.6 56.7 %copy-start.6 = (s32[128]{0:T(128)}, s32[128]{0:T(128)S(1)}, u32[]{:S(2)}) copy-start(s32[128]{0:T(128)S(1)} %reshape.186) | copy-start | bytes 1540
  28.8 4.3 copy-start.1
  33.1 17.7 %slice-start = ((s8[8388608]{0:T(1024)(128)(4,1)}), s8[4194304]{0:T(1024)(128)(4,1)S(1)}, s32[]{:S(2)}) async-start(s8[8388608]{0:T(1024)(128)(4,1)} %bitcast.126), calls=%async_computation.1 | async-start | bytes 8388608
  33.8 17.1 %slice-start.1 = ((s8[8388608]{0:T(1024)(128)(4,1)}), s8[4194304]{0:T(1024)(128)(4,1)S(1)}, s32[]{:S(2)}) async-start(s8[8388608]{0:T(1024)(128)(4,1)} %bitcast.126), calls=%async_computation.2 | async-start | bytes 8388608
  279.8 1.2 copy-start.3
  283.8 3.7 collective-permute-start.1
  285.6 5.9 collective-permute-start.2
  291.6 27.1 %collective-permute-start.3 = (f32[16,10,1,128]{3,0,2,1:T(8,128)S(1)}, f32[16,10,1,128]{3,0,2,1:T(8,128)S(1)}, u32[]{:S(2)}, u32[]{:S(2)}) collective-permute-start(f32[16,10,1,128]{3,0,2,1:T(8,128)S(1)} %get-tuple-element.44), channel_id=1, source_target_pairs={{0,1},{1,2},{2,3},{3,4},{4,5},{5,6},{6,7},{8,9},{9,10},{10,11},{11... | collective-permute-start | bytes 245768 | tf_op jit(solution)/shard_map/ppermute | solution.py:19
  301.4 17.3 %collective-permute-start.4 = (f32[16,10,1,128]{3,0,2,1:T(8,128)S(1)}, f32[16,10,1,128]{3,0,2,1:T(8,128)S(1)}, u32[]{:S(2)}, u32[]{:S(2)}) collective-permute-start(f32[16,10,1,128]{3,0,2,1:T(8,128)S(1)} %get-tuple-element.45), channel_id=1, source_target_pairs={{1,0},{2,1},{3,2},{4,3},{5,4},{6,5},{7,6},{9,8},{10,9},{11,10},{12... | collective-permute-start | bytes 245768 | tf_op jit(solution)/shard_map/ppermute | solution.py:20
  397.6 2.1 copy-start.7
  397.6 2.1 copy-start.4
  397.6 17.9 %slice-start.2 = ((s8[8388608]{0:T(1024)(128)(4,1)}), s8[4194304]{0:T(1024)(128)(4,1)S(1)}, s32[]{:S(2)}) async-start(s8[8388608]{0:T(1024)(128)(4,1)} %bitcast.128), calls=%async_computation.3 | async-start | bytes 8388608
  399.7 15.8 %slice-start.3 = ((s8[8388608]{0:T(1024)(128)(4,1)}), s8[4194304]{0:T(1024)(128)(4,1)S(1)}, s32[]{:S(2)}) async-start(s8[8388608]{0:T(1024)(128)(4,1)} %bitcast.128), calls=%async_computation.4 | async-start | bytes 8388608
  415.5 234.7 %copy-start.2 = (f32[128,16,128]{2,1,0:T(8,128)}, f32[128,16,128]{2,1,0:T(8,128)S(1)}, u32[]{:S(2)}) copy-start(f32[128,16,128]{2,1,0:T(8,128)S(1)} %get-tuple-element.72) | copy-start | bytes 3145732
  652.9 108.0 %copy-start.5 = (f32[16]{0:T(128)S(1)}, f32[16]{0:T(128)}, u32[]{:S(2)}) copy-start(f32[16]{0:T(128)} %copy-done.4) | copy-start | bytes 196
  652.9 5.8 collective-permute-start.5
  656.6 5.7 collective-permute-start.6
  662.3 21.6 %collective-permute-start.7 = (f32[16,10,1,128]{3,0,2,1:T(8,128)S(1)}, f32[16,10,1,128]{3,0,2,1:T(8,128)S(1)}, u32[]{:S(2)}, u32[]{:S(2)}) collective-permute-start(f32[16,10,1,128]{3,0,2,1:T(8,128)S(1)} %get-tuple-element.42), channel_id=1, source_target_pairs={{0,1},{1,2},{2,3},{3,4},{4,5},{5,6},{6,7},{8,9},{9,10},{10,11},{11... | collective-permute-start | bytes 245768 | tf_op jit(solution)/shard_map/ppermute | solution.py:19
  666.6 17.3 %collective-permute-start.8 = (f32[16,10,1,128]{3,0,2,1:T(8,128)S(1)}, f32[16,10,1,128]{3,0,2,1:T(8,128)S(1)}, u32[]{:S(2)}, u32[]{:S(2)}) collective-permute-start(f32[16,10,1,128]{3,0,2,1:T(8,128)S(1)} %get-tuple-element.43), channel_id=1, source_target_pairs={{1,0},{2,1},{3,2},{4,3},{5,4},{6,5},{7,6},{9,8},{10,9},{11,10},{12... | collective-permute-start | bytes 245768 | tf_op jit(solution)/shard_map/ppermute | solution.py:20
Sparse Core Ops, SparseCore 0:
  71.9 146.2 all-reduce.4
where the time goes:
time: 779 us; the launch traced here: 772 us
  blocking collectives  484 us (62%)
  matrix products  97.2 us (12%)
  other arithmetic  82.4 us (11%)
  waiting for transfers between devices  32.7 us (4%)
  local copies, waits for them, and re-layouts  30.2 us (4%)
  starting transfers between devices  27.3 us (4%)
  between operations  18.8 us (2%)
    psum x2, blocking collectives, coarse_part(): gathered = lax.psum(local, 'row')  231 us
    psum x2, blocking collectives, alignment_sum(): return lax.psum(jnp.sum(residual * zeta, axis=(1, 2, 3)), ('row', 'col'))  177 us
    dot_general x6, matrix products, block_products(): jnp.einsum('bij,sbj->sbi', picked, flat, precision=lax.Precision.HIGHEST)  91.1 us
    psum x1, blocking collectives, on_device(): lax.psum(jnp.sum(direction * image, axis=(1, 2, 3)), ('row', 'col'))  75.4 us
    another operation x6, other arithmetic, on_device(): factor = jnp.linalg.cholesky(coarse_matrix)  33.9 us
    psum x1, waiting for transfers between devices, on_device(): coarse_matrix = lax.psum(local_matrix + cross_matrix, 'row')  23.6 us
    another operation x6, other arithmetic, coarse_part(): solved = jax.scipy.linalg.cho_solve((factor, True), gathered)  19.9 us
    ppermute x4, starting transfers between devices, padded_2(): before = lax.ppermute(last, axis, up)  19.5 us
  transfers between devices with their start and end apart: 10, of which 5 were waited for; matrix products, arithmetic and copies ran while one was open for 11% of the time, Pallas kernels for 0%

commit v1 on v0

v1 whole, which is shorter than its diff:
```python
import functools
import jax
import jax.numpy as jnp
from jax import lax
from jax.experimental import pallas as pl
from jax.experimental.pallas import tpu as pltpu
from jax.sharding import PartitionSpec as P

MESH = pl.DeviceIdType.MESH
F32 = jnp.float32
BF = jnp.bfloat16
LAST = (((1,), (1,)), ((), ()))
PLAIN = (((1,), (0,)), ((), ()))
NEWTON = 6
REFINE = 2
AGR = 4
AGC = 4


def iota(shape, dim):
    return lax.broadcasted_iota(jnp.int32, shape, dim)


def onehot(mask):
    return jnp.where(mask, 1.0, 0.0).astype(BF)


def split2(x):
    hi = x.astype(BF)
    lo = (x - hi.astype(F32)).astype(BF)
    return hi, lo


def split3(x):
    hi = x.astype(BF)
    rest = x - hi.astype(F32)
    mid = rest.astype(BF)
    lo = (rest - mid.astype(F32)).astype(BF)
    return hi, mid, lo


def dot(a, b, dims=PLAIN):
    return lax.dot_general(a, b, dims, preferred_element_type=F32)


def rows_dot(x, table, dims):
    m = x.shape[0]
    y = dot(jnp.concatenate(split3(x), axis=0), table, dims)
    return y[:m] + y[m : 2 * m] + y[2 * m :]


def cols_dot(table, x):
    m = x.shape[0]
    y = dot(table, jnp.concatenate(split3(x), axis=0), LAST)
    return y[:, :m] + y[:, m : 2 * m] + y[:, 2 * m :]


def kernel(
    n_r, n_c,
    r_ref, lib_ref, strap_ref, typ_ref, ids_ref,
    v_ref, res_ref,
    z_ref, u_ref, w_ref, t_ref,
    lib_w, inv_t, cop_t, typ_t, rs_t,
    own_idt, gat_idt, own_rho, gat_rho, own_tau, gat_tau,
    idsh, oh_all, acc, dacc, mat, mat_h, xmat,
    edge_out, halo_ns, halo_ew,
    cedge_out, cedge_in,
    dots, own_sum, row_sum, own_col, col_sum,
    send_idt, recv_idt, send_rho, recv_rho, send_tau, recv_tau,
    send_halo, recv_halo, send_edge, recv_edge,
    send_rs, recv_rs, send_cs, recv_cs,
):
    sz, rl, cl, nd = r_ref.shape
    nb = rl * cl
    nt = lib_ref.shape[0]
    ng = acc.shape[0]
    me = lax.axis_index("row")
    mc = lax.axis_index("col")

    def row_peer(off):
        return {"row": lax.rem(me + off, n_r)}

    def col_peer(off):
        return {"col": lax.rem(mc + off, n_c)}

    barrier = pltpu.get_barrier_semaphore()

    def greet_row(off, carry):
        pl.semaphore_signal(barrier, inc=1, device_id=row_peer(off), device_id_type=MESH)
        return carry

    def greet_col(off, carry):
        pl.semaphore_signal(barrier, inc=1, device_id=col_peer(off), device_id_type=MESH)
        return carry

    lax.fori_loop(1, n_r, greet_row, 0)
    lax.fori_loop(1, n_c, greet_col, 0)

    strap0 = strap_ref[0:1, :]
    strap1 = strap_ref[1:2, :]
    couple = 2.0 * strap0 + 2.0 * strap1
    nw = jnp.sum(strap0, axis=1, keepdims=True)
    ew = jnp.sum(strap1, axis=1, keepdims=True)
    eye = iota((nd, nd), 0) == iota((nd, nd), 1)
    spread = onehot(iota((cl, nb), 0) == lax.rem(iota((cl, nb), 1), cl))
    mine = iota((rl, nb), 0) == iota((rl, nb), 1) // cl

    def flat_row(ref):
        wide = dot(ref[...].astype(F32).astype(BF), spread)
        return jnp.sum(jnp.where(mine, wide, 0.0), axis=0, keepdims=True)

    id_row = flat_row(ids_ref)
    typ_row = flat_row(typ_ref)
    own_idt[0:1, :] = id_row
    own_idt[1:2, :] = typ_row

    def column(row):
        return jnp.transpose(jnp.broadcast_to(row, (nb, nb)))

    typ = column(typ_row)
    typ_t[...] = typ
    diag = jnp.zeros((nb, nd), F32)
    rsum = jnp.zeros((nb, nd), F32)
    sums = []
    for t in range(nt):
        lib = lib_ref[t]
        hi, lo = split2(lib)
        half = (t % 2) * nd
        lib_w[t // 2, 0:nd, half : half + nd] = hi
        lib_w[t // 2, nd : 2 * nd, half : half + nd] = hi
        lib_w[t // 2, 2 * nd : 3 * nd, half : half + nd] = lo
        rows = jnp.sum(lib, axis=0, keepdims=True)
        sums.append(jnp.sum(rows, axis=1, keepdims=True))
        diag = jnp.where(typ == t, jnp.sum(jnp.where(eye, lib, 0.0), axis=0, keepdims=True), diag)
        rsum = jnp.where(typ == t, rows, rsum)
    inv_t[...] = 1.0 / (diag + couple)
    cop_t[...] = jnp.broadcast_to(couple, (nb, nd))
    rs_t[...] = rsum + couple

    def block_products(x):
        k = x.shape[0] // nb
        hi, lo = split2(x)
        wide = jnp.concatenate([hi, lo, hi], axis=1)
        types = jnp.concatenate([typ_t[...]] * k, axis=0)
        out = jnp.zeros(x.shape, F32)
        for pair in range(nt // 2):
            both = dot(wide, lib_w[pair])
            out = jnp.where(types == 2 * pair, both[:, :nd], out)
            out = jnp.where(types == 2 * pair + 1, both[:, nd:], out)
        return out

    chunk = 4

    def load(ref, i):
        return ref[pl.ds(i * chunk, chunk)].reshape(chunk * nb, nd)

    def store(ref, i, value):
        ref[pl.ds(i * chunk, chunk)] = value.reshape(chunk, rl, cl, nd)

    def smooth(src, dst):
        def body(i, carry):
            v = load(src, i)
            inv = jnp.concatenate([inv_t[...]] * chunk, axis=0)
            y = v * inv
            for sweep in range(2):
                y = y + (v - block_products(y) - couple * y) * inv
            store(dst, i, y)
            return carry

        lax.fori_loop(0, sz // chunk, body, 0)

    ones = jnp.ones((8, 3 * nd), BF)

    def block_sums(src, dst):
        def body(i, carry):
            x = load(src, i)
            wide = jnp.concatenate(split3(x), axis=1)
            y = dot(ones, wide, LAST)
            for j in range(chunk):
                dst[pl.ds(i * chunk + j, 1), :] = y[0:1, j * nb : (j + 1) * nb]
            return carry

        lax.fori_loop(0, sz // chunk, body, 0)

    def put_row(own, gathered, send, recv):
        def body(off, carry):
            pltpu.make_async_remote_copy(
                src_ref=own,
                dst_ref=gathered.at[me],
                send_sem=send,
                recv_sem=recv,
                device_id=row_peer(off),
                device_id_type=MESH,
            ).start()
            return carry

        lax.fori_loop(1, n_r, body, 0)
        gathered[pl.ds(me, 1)] = own[...][None]

    def wait_bytes(gathered, sem, count):
        part = gathered.at[pl.ds(0, count)]
        pltpu.make_async_copy(part, part, sem).wait()

    block_sums(r_ref, own_rho)
    smooth(r_ref, z_ref)

    pl.semaphore_wait(barrier, n_r - 1 + n_c - 1)
    put_row(own_idt, gat_idt, send_idt, recv_idt)

    north, south = me - 1, me + 1
    west, east = mc - 1, mc + 1
    has = (me > 0, me < n_r - 1, mc > 0, mc < n_c - 1)

    def halo_copies(rnd, src):
        where = ({"row": north}, {"row": south}, {"col": west}, {"col": east})
        sources = (src.at[:, 0], src.at[:, rl - 1], edge_out.at[rnd, 0], edge_out.at[rnd, 1])
        targets = (halo_ns.at[rnd, 1], halo_ns.at[rnd, 0], halo_ew.at[rnd, 1], halo_ew.at[rnd, 0])
        landing = (halo_ns.at[rnd, 0], halo_ns.at[rnd, 1], halo_ew.at[rnd, 0], halo_ew.at[rnd, 1])
        came = (1, 0, 3, 2)
        out = []
        for k in range(4):
            give = pltpu.make_async_remote_copy(
                src_ref=sources[k],
                dst_ref=targets[k],
                send_sem=send_halo.at[rnd, k],
                recv_sem=recv_halo.at[rnd, k],
                device_id=where[k],
                device_id_type=MESH,
            )
            take = pltpu.make_async_copy(landing[k], landing[k], recv_halo.at[rnd, came[k]])
            out.append((has[k], give, take, landing[k]))
        return out

    def halo_start(rnd, src):
        edge_out[rnd, 0] = src[:, :, 0, :]
        edge_out[rnd, 1] = src[:, :, cl - 1, :]
        for here, give, _, landing in halo_copies(rnd, src):

            @pl.when(here)
            def _():
                give.start()

            @pl.when(jnp.logical_not(here))
            def _():
                landing[...] = jnp.zeros(landing.shape, F32)

    def halo_wait(rnd, src):
        for here, give, take, _ in halo_copies(rnd, src):

            @pl.when(here)
            def _():
                take.wait()
                give.wait_send()

    halo_start(0, z_ref)
    put_row(own_rho, gat_rho, send_rho, recv_rho)

    def products(src, dst):
        def body(i, carry):
            store(dst, i, block_products(load(src, i)))
            return carry

        lax.fori_loop(0, sz // chunk, body, 0)

    def lateral(rnd, src, s):
        f = src[s]
        up = halo_ns[rnd, 0, s][None]
        down = halo_ns[rnd, 1, s][None]
        fn = jnp.concatenate([up, f[:-1]], axis=0)
        fs = jnp.concatenate([f[1:], down], axis=0)
        left = halo_ew[rnd, 0, s][:, None, :]
        right = halo_ew[rnd, 1, s][:, None, :]
        fw = jnp.concatenate([left, f[:, :-1]], axis=1)
        fe = jnp.concatenate([f[:, 1:], right], axis=1)
        return strap0 * (2.0 * f - fn - fs) + strap1 * (2.0 * f - fw - fe)

    products(z_ref, u_ref)
    halo_wait(0, z_ref)

    def add_lateral(s, carry):
        u_ref[s] = u_ref[s] + lateral(0, z_ref, s)
        return carry

    lax.fori_loop(0, sz, add_lateral, 0)
    block_sums(u_ref, own_tau)
    put_row(own_tau, gat_tau, send_tau, recv_tau)

    wait_bytes(gat_idt, recv_idt, n_r - 1)
    ids = gat_idt[:, 0, :]
    typs = gat_idt[:, 1, :]
    lane = iota((n_r, nb), 1)
    dev = iota((n_r, nb), 0)
    none = jnp.full((1, nb), -1.0, F32)
    above = jnp.concatenate([none, ids[:-1]], axis=0)
    below = jnp.concatenate([ids[1:], none], axis=0)
    idsh[0] = ids
    idsh[1] = jnp.where(lane < cl, pltpu.roll(above, cl, 1), pltpu.roll(ids, cl, 1))
    idsh[2] = jnp.where(lane >= nb - cl, pltpu.roll(below, nb - cl, 1), pltpu.roll(ids, nb - cl, 1))
    idsh[3] = jnp.where(lax.rem(lane, cl) == 0, -1.0, pltpu.roll(ids, 1, 1))
    idsh[4] = jnp.where(lax.rem(lane, cl) == cl - 1, -1.0, pltpu.roll(ids, nb - 1, 1))
    centre = jnp.zeros((n_r, nb), F32)
    for t in range(nt):
        centre = jnp.where(typs == t, sums[t], centre)
    idsh[5] = centre + 2.0 * nw + 2.0 * ew

    acc[...] = jnp.zeros(acc.shape, F32)
    dacc[...] = jnp.zeros(dacc.shape, F32)
    agg = iota((ng, 2 * nb), 0).astype(F32)

    def assemble(k, carry):
        def pair(j):
            return jnp.concatenate(
                [idsh[j, pl.ds(2 * k, 1), :], idsh[j, pl.ds(2 * k + 1, 1), :]], axis=1
            )

        here = agg == pair(0)
        mask = onehot(here)
        oh_all[k] = mask
        other = jnp.concatenate([onehot(agg == pair(2)), onehot(agg == pair(4))], axis=0)
        acc[...] += dot(mask, other, LAST)
        weighted = jnp.where(here, pair(5), 0.0)
        dacc[...] += weighted[:, :nb] + weighted[:, nb:]
        return carry

    lax.fori_loop(0, n_r // 2, assemble, 0)
    big_eye = iota((ng, ng), 0) == iota((ng, ng), 1)
    cross = nw * acc[:, :ng] + ew * acc[:, ng:]
    total = jnp.sum(dacc[...], axis=1, keepdims=True)
    coarse = jnp.where(big_eye, total, 0.0) - cross - jnp.transpose(cross)
    on_diag = jnp.where(big_eye, coarse, 0.0)
    scale = lax.rsqrt(jnp.sum(on_diag, axis=0, keepdims=True))
    scaled = coarse * scale * lax.rsqrt(jnp.sum(on_diag, axis=1, keepdims=True))
    a_hi, a_mid, a_lo = split3(scaled)
    mat[0] = a_hi
    mat[1] = a_mid
    mat[2] = a_lo
    mat_h[:, 0:ng] = a_hi
    mat_h[:, ng : 2 * ng] = a_mid
    mat_h[:, 2 * ng : 3 * ng] = a_hi

    low = jnp.broadcast_to(0.0085 * ew / (nw + ew), (1, ng))
    mu = 2.0 / (1.0 + low)
    xmat[...] = jnp.where(big_eye, mu, 0.0) - (0.25 * mu * mu) * scaled
    low = 4.0 * low / ((1.0 + low) * (1.0 + low))

    def newton(i, low):
        mu = 2.0 / (1.0 + low)
        x = xmat[...]
        x_hi, x_lo = split2(x)
        t_hi, t_lo = split2(dot(mat_h[...], jnp.concatenate([x_hi, x_hi, x_lo], axis=0)))
        xt = dot(
            jnp.concatenate([x_hi, x_lo, x_hi], axis=1),
            jnp.concatenate([t_hi, t_hi, t_lo], axis=0),
        )
        xmat[...] = 2.0 * mu * x - (mu * mu) * xt
        return 4.0 * low / ((1.0 + low) * (1.0 + low))

    lax.fori_loop(0, NEWTON, newton, low)
    inv_hi, inv_lo = split2(xmat[...])

    def by_inverse(g):
        y = dot(jnp.concatenate(split2(g), axis=0), inv_hi)
        return y[:sz] + y[sz:] + dot(g.astype(BF), inv_lo)

    def by_matrix(c):
        c_hi, c_mid, c_lo = split3(c)
        y = dot(jnp.concatenate([c_hi, c_mid, c_lo], axis=0), mat[0])
        x = dot(jnp.concatenate([c_hi, c_mid], axis=0), mat[1])
        return (y[2 * sz :] + x[sz:] + dot(c_hi, mat[2])) + (y[sz : 2 * sz] + x[:sz]) + y[:sz]

    def solve(g):
        g = g * scale
        c = by_inverse(g)
        for _ in range(REFINE):
            c = c + by_inverse(g - by_matrix(c))
        return c * scale

    def aggregate(gathered):
        def body(k, total):
            x = jnp.concatenate([gathered[2 * k], gathered[2 * k + 1]], axis=1)
            return total + rows_dot(x, oh_all[k], LAST)

        return lax.fori_loop(0, n_r // 2, body, jnp.zeros((sz, ng), F32))

    wait_bytes(gat_rho, recv_rho, n_r - 1)
    sums_r = aggregate(gat_rho)
    c = solve(sums_r)

    pick = iota((nb, nb), 0)
    slot = iota((nb, nb), 1)
    first = dot(ids.astype(BF), onehot(pick == slot * cl))
    final = dot(ids.astype(BF), onehot(pick == slot * cl + cl - 1))
    agg_lane = iota((n_r, ng), 1).astype(F32)
    oh_first = jnp.concatenate([onehot(first[:, j : j + 1] == agg_lane) for j in range(rl)], axis=0)
    oh_final = jnp.concatenate([onehot(final[:, j : j + 1] == agg_lane) for j in range(rl)], axis=0)
    cedge_out[0] = rows_dot(c, oh_first, LAST)
    cedge_out[1] = rows_dot(c, oh_final, LAST)

    def edge_copies():
        out = []
        for k, to in ((0, west), (1, east)):
            give = pltpu.make_async_remote_copy(
                src_ref=cedge_out.at[k],
                dst_ref=cedge_in.at[1 - k],
                send_sem=send_edge.at[k],
                recv_sem=recv_edge.at[k],
                device_id={"col": to},
                device_id_type=MESH,
            )
            take = pltpu.make_async_copy(cedge_in.at[k], cedge_in.at[k], recv_edge.at[1 - k])
            out.append((has[2 + k], give, take, cedge_in.at[k]))
        return out

    for here, give, _, landing in edge_copies():

        @pl.when(here)
        def _():
            give.start()

        @pl.when(jnp.logical_not(here))
        def _():
            landing[...] = jnp.zeros(landing.shape, F32)

    wide_lane = iota((nb, ng), 1).astype(F32)

    def local_onehot(j):
        col = column(idsh[j, pl.ds(me, 1), :])
        return jnp.concatenate([col] * (ng // nb), axis=1) == wide_lane

    oh_own = onehot(local_onehot(0))
    oh_ns = onehot(local_onehot(1)) + onehot(local_onehot(2))
    oh_we = onehot(local_onehot(3)) + onehot(local_onehot(4))
    c_own = cols_dot(oh_own, c)
    c_ns = cols_dot(oh_ns, c)
    c_we = cols_dot(oh_we, c)
    wait_bytes(gat_tau, recv_tau, n_r - 1)
    sums_u = aggregate(gat_tau) + sums_r

    for here, give, take, _ in edge_copies():

        @pl.when(here)
        def _():
            take.wait()
            give.wait_send()

    block = iota((nb, ng), 0)
    spot = iota((nb, ng), 1) == (block // cl) * n_r + me
    at_west = onehot(jnp.logical_and(lax.rem(block, cl) == 0, spot))
    at_east = onehot(jnp.logical_and(lax.rem(block, cl) == cl - 1, spot))
    from_west = cedge_in[0]
    from_east = cedge_in[1]
    c_we = c_we + cols_dot(at_west, from_west) + cols_dot(at_east, from_east)
    over = rows_dot(from_west, oh_first, PLAIN) + rows_dot(from_east, oh_final, PLAIN)
    d = solve(sums_u - ew * over)
    d_own = cols_dot(oh_own, d)

    rs = rs_t[...]
    for s in range(sz):
        own = c_own[:, s : s + 1]
        image = own * rs - c_ns[:, s : s + 1] * strap0 - c_we[:, s : s + 1] * strap1
        z_ref[s] = z_ref[s] + jnp.broadcast_to(own, (nb, nd)).reshape(rl, cl, nd)
        u_ref[s] = u_ref[s] + image.reshape(rl, cl, nd)

    smooth(u_ref, w_ref)
    for s in range(sz):
        w_ref[s] = w_ref[s] + jnp.broadcast_to(d_own[:, s : s + 1], (nb, nd)).reshape(rl, cl, nd)
    halo_start(1, w_ref)
    products(w_ref, t_ref)
    halo_wait(1, w_ref)

    def finish(s, carry):
        r, z, u, w = r_ref[s], z_ref[s], u_ref[s], w_ref[s]
        t = t_ref[s] + lateral(1, w_ref, s)
        t_ref[s] = t
        for k, (a, b) in enumerate(((r, z), (z, u), (r, w), (u, w), (z, t), (w, t))):
            part = jnp.sum((a * b).reshape(nb, nd), axis=0, keepdims=True)
            dots[k, pl.ds(s, 1), :] = part
        return carry

    lax.fori_loop(0, sz, finish, 0)

    lane_s = iota((sz, nd), 1)
    row_s = iota((sz, nd), 0)
    packed = jnp.zeros((sz, nd), F32)
    for k in range(6):
        value = jnp.sum(dots[k], axis=1, keepdims=True)
        packed = packed + jnp.where(lane_s == row_s * 8 + k, value, 0.0)
    own_sum[...] = jnp.sum(packed, axis=0, keepdims=True)
    put_row(own_sum, row_sum, send_rs, recv_rs)
    wait_bytes(row_sum, recv_rs, n_r - 1)
    own_col[...] = jnp.sum(row_sum[...], axis=0)

    def put_col(off, carry):
        pltpu.make_async_remote_copy(
            src_ref=own_col,
            dst_ref=col_sum.at[mc],
            send_sem=send_cs,
            recv_sem=recv_cs,
            device_id=col_peer(off),
            device_id_type=MESH,
        ).start()
        return carry

    lax.fori_loop(1, n_c, put_col, 0)
    col_sum[pl.ds(mc, 1)] = own_col[...][None]
    wait_bytes(col_sum, recv_cs, n_c - 1)
    every = jnp.broadcast_to(jnp.sum(col_sum[...], axis=0), (sz, nd))

    def unpack(k):
        return jnp.sum(jnp.where(lane_s == row_s * 8 + k, every, 0.0), axis=1, keepdims=True)

    rz, zu, rw, uw, zt, wt = [unpack(k) for k in range(6)]
    step0 = rz / zu
    fresh = rz - step0 * (rw + zu) + step0 * step0 * uw
    blend1 = 1.0 + fresh / rz
    curv = blend1 * blend1 * zu - blend1 * step0 * (zt + uw) + step0 * step0 * wt
    step1 = fresh / curv
    on_first = step0 + step1 * blend1
    on_second = step0 * step1
    dots[0] = jnp.broadcast_to(on_first, (sz, nd))
    dots[1] = jnp.broadcast_to(on_second, (sz, nd))

    def output(s, carry):
        a = dots[0, pl.ds(s, 1), :]
        b = dots[1, pl.ds(s, 1), :]
        v_ref[s] = a * z_ref[s] - b * w_ref[s]
        res_ref[s] = r_ref[s] - a * u_ref[s] + b * t_ref[s]
        return carry

    lax.fori_loop(0, sz, output, 0)

    wait_bytes(gat_idt, send_idt, n_r - 1)
    wait_bytes(gat_rho, send_rho, n_r - 1)
    wait_bytes(gat_tau, send_tau, n_r - 1)
    wait_bytes(row_sum, send_rs, n_r - 1)
    wait_bytes(col_sum, send_cs, n_c - 1)


def on_device(n_r, n_c, load_currents, block_library, strap_conductance, block_types, aggregate_map):
    sz, rl, cl, nd = load_currents.shape
    nt = block_library.shape[0]
    nb = rl * cl
    ng = n_r * rl // AGR * (cl // AGC)
    vmem = pl.BlockSpec(memory_space=pltpu.VMEM)
    field = pltpu.VMEM((sz, rl, cl, nd), F32)
    shape = jax.ShapeDtypeStruct(load_currents.shape, F32)
    dma = pltpu.SemaphoreType.DMA
    table = pltpu.VMEM((nb, nd), F32)
    return pl.pallas_call(
        functools.partial(kernel, n_r, n_c),
        out_shape=(shape, shape),
        in_specs=[vmem] * 5,
        out_specs=(vmem, vmem),
        scratch_shapes=[
            field, field, field, field,
            pltpu.VMEM((nt // 2, 3 * nd, 2 * nd), BF), table, table, table, table,
            pltpu.VMEM((2, nb), F32), pltpu.VMEM((n_r, 2, nb), F32),
            pltpu.VMEM((sz, nb), F32), pltpu.VMEM((n_r, sz, nb), F32),
            pltpu.VMEM((sz, nb), F32), pltpu.VMEM((n_r, sz, nb), F32),
            pltpu.VMEM((6, n_r, nb), F32), pltpu.VMEM((n_r // 2, ng, 2 * nb), BF),
            pltpu.VMEM((ng, 2 * ng), F32), pltpu.VMEM((ng, nb), F32),
            pltpu.VMEM((3, ng, ng), BF), pltpu.VMEM((ng, 3 * ng), BF), pltpu.VMEM((ng, ng), F32),
            pltpu.VMEM((2, 2, sz, rl, nd), F32), pltpu.VMEM((2, 2, sz, cl, nd), F32),
            pltpu.VMEM((2, 2, sz, rl, nd), F32),
            pltpu.VMEM((2, sz, ng), F32), pltpu.VMEM((2, sz, ng), F32),
            pltpu.VMEM((6, sz, nd), F32), pltpu.VMEM((1, nd), F32), pltpu.VMEM((n_r, 1, nd), F32),
            pltpu.VMEM((1, nd), F32), pltpu.VMEM((n_c, 1, nd), F32),
            dma, dma, dma, dma, dma, dma,
            dma((2, 4)), dma((2, 4)), dma((2,)), dma((2,)),
            dma, dma, dma, dma,
        ],
        compiler_params=pltpu.CompilerParams(
            collective_id=0, has_side_effects=True, vmem_limit_bytes=56 * 1024 * 1024
        ),
    )(load_currents, block_library, strap_conductance, block_types, aggregate_map)


def solution(mesh):
    placed = (P(None, "row", "col", None), P(), P(), P("row", "col"), P("row", "col"))
    return jax.shard_map(
        functools.partial(on_device, mesh.shape["row"], mesh.shape["col"]),
        mesh=mesh,
        in_specs=placed,
        out_specs=(P(None, "row", "col", None), P(None, "row", "col", None)),
        check_vma=False,
    )
```

time: 779 us -> 70.5 us (0.09)
  blocking collectives: 484 us -> 0 us
  matrix products: 97.2 us -> 0 us
  other arithmetic: 82.4 us -> 0 us
  Pallas kernels: 0 us -> 66.3 us
  waiting for transfers between devices: 32.7 us -> 0 us
  starting transfers between devices: 27.3 us -> 0 us
  local copies, waits for them, and re-layouts: 30.2 us -> 3.36 us
  between operations: 18.8 us -> 0.65 us
    psum x5 -> x0, blocking collectives: 484 us -> none  [the longest x2 231 us: coarse_part(): gathered = lax.psum(local, 'row')]
    dot_general x6 -> x0, matrix products: 91.1 us -> none  [block_products(): jnp.einsum('bij,sbj->sbi', picked, flat, precision=lax.Precision.HIGHEST)]
    pallas_call x0 -> x1, Pallas kernels: none -> 66.3 us  [on_device(): pl.pallas_call(functools.partial(kernel, n_r, n_c), out_shape=(shape, sha...]
    another operation x13 -> x0, other arithmetic: 54 us -> none  [the longest x6 33.9 us: on_device(): factor = jnp.linalg.cholesky(coarse_matrix)]
    ppermute x9 -> x0, starting transfers between devices: 27.2 us -> none  [the longest x4 19.5 us: padded_2(): before = lax.ppermute(last, axis, up)]
    psum x1 -> x0, waiting for transfers between devices: 23.6 us -> none  [on_device(): coarse_matrix = lax.psum(local_matrix + cross_matrix, 'row')]
    add x11 -> x0, other arithmetic: 11 us -> none  [the longest x1 4.71 us: on_device(): coarse_matrix = lax.psum(local_matrix + cross_matrix, 'row')]
    gather x7 -> x0, local copies, waits for them, and re-layouts: 9.34 us -> none  [the longest x1 4.31 us: on_device(): picked = block_library[block_types.reshape(-1)]]
  transfers between devices with their start and end apart: 10 -> 0, of which waited for: 5 -> 0; matrix products, arithmetic and copies ran while one was open for 11% -> 0% of each run, Pallas kernels for 0% -> 0%
where the time goes in v1:
time: 70.5 us; the launch traced here: 70.3 us
  Pallas kernels  66.3 us (94%)
  local copies, waits for them, and re-layouts  3.36 us (5%)
    pallas_call x1, Pallas kernels, on_device(): pl.pallas_call(functools.partial(kernel, n_r, n_c), out_shape=(shape, sha...  66.3 us
    unnamed x4, local copies, waits for them, and re-layouts  3.36 us

profile of v1, /device:TPU:1, one launch (start us, length us, event | category | flops | bytes accessed | tf_op | source)
XLA Modules:
  0.0 70.3 jit_solution(11288563449451891532)
XLA Ops:
  0.6 66.3 %shard_map.68 = (f32[16,8,16,128]{3,2,1,0:T(8,128)}, f32[16,8,16,128]{3,2,1,0:T(8,128)}) custom-call(f32[16,8,16,128]{3,2,1,0:T(8,128)} %r_ref.1, f32[8,128,128]{2,1,0:T(8,128)} %lib_ref.1, f32[2,128]{1,0:T(2,128)} %strap_ref.1, s32[8,16]{1,0:T(8,128)} %typ_ref.1, s32[8,16]{1,0:T(8,128)} %ids_ref.1), custom_call_target="tpu_custom_call" | custom-call | tf_op jit(solution)/shard_map/pallas_call | solution.py:549
  67.0 0.0 copy-start
  67.0 2.4 %copy.9 = f32[16,8,16,128]{3,2,1,0:T(8,128)} copy(f32[16,8,16,128]{3,2,1,0:T(8,128)} %get-tuple-element.4) | data formatting | bytes 2097152
  69.4 0.0 copy-done
  69.4 1.0 %copy.10 = f32[16,8,16,128]{3,2,1,0:T(8,128)} copy(f32[16,8,16,128]{3,2,1,0:T(8,128)S(1)} %copy-done) | data formatting | bytes 2097152
Async XLA Ops:
  67.0 2.4 %copy-start = (f32[16,8,16,128]{3,2,1,0:T(8,128)S(1)}, f32[16,8,16,128]{3,2,1,0:T(8,128)}, u32[]{:S(2)}) copy-start(f32[16,8,16,128]{3,2,1,0:T(8,128)} %get-tuple-element.5) | copy-start | bytes 3145732

commit v2 on v1

v2 whole, which is shorter than its diff:
```python
import functools
import jax
import jax.numpy as jnp
from jax import lax
from jax.experimental import pallas as pl
from jax.experimental.pallas import tpu as pltpu
from jax.sharding import PartitionSpec as P

MESH = pl.DeviceIdType.MESH
F32 = jnp.float32
BF = jnp.bfloat16
LAST = (((1,), (1,)), ((), ()))
PLAIN = (((1,), (0,)), ((), ()))
NEWTON = 6
REFINE = 2
AGR = 4
AGC = 4
GROUP = 8
UNROLL = 4
STEP = 4


def iota(shape, dim):
    return lax.broadcasted_iota(jnp.int32, shape, dim)


def onehot(mask):
    return jnp.where(mask, 1.0, 0.0).astype(BF)


def split2(x):
    hi = x.astype(BF)
    lo = (x - hi.astype(F32)).astype(BF)
    return hi, lo


def split3(x):
    hi = x.astype(BF)
    rest = x - hi.astype(F32)
    mid = rest.astype(BF)
    lo = (rest - mid.astype(F32)).astype(BF)
    return hi, mid, lo


def dot(a, b, dims=PLAIN):
    return lax.dot_general(a, b, dims, preferred_element_type=F32)


def rows_dot(x, table, dims):
    m = x.shape[0]
    y = dot(jnp.concatenate(split3(x), axis=0), table, dims)
    return y[:m] + y[m : 2 * m] + y[2 * m :]


def cols_dot(table, x):
    m = x.shape[0]
    y = dot(table, jnp.concatenate(split3(x), axis=0), LAST)
    return y[:, :m] + y[:, m : 2 * m] + y[:, 2 * m :]


def flat_row(ref, rl, cl):
    nb = rl * cl
    spread = onehot(iota((cl, nb), 0) == lax.rem(iota((cl, nb), 1), cl))
    mine = iota((rl, nb), 0) == iota((rl, nb), 1) // cl
    wide = dot(ref[...].astype(F32).astype(BF), spread)
    return jnp.sum(jnp.where(mine, wide, 0.0), axis=0, keepdims=True)


def order_kernel(nt, typ_ref, idx_v):
    rl, cl = typ_ref.shape
    nb = rl * cl
    typ_row = flat_row(typ_ref, rl, cl)

    one_type = iota((nt, nb), 0).astype(F32) == typ_row
    before = dot(onehot(one_type), onehot(iota((nb, nb), 0) < iota((nb, nb), 1)))
    members = jnp.sum(jnp.where(one_type, 1.0, 0.0), axis=1, keepdims=True)
    groups = jnp.floor((members + (GROUP - 1)) * (1.0 / GROUP))
    start = jnp.zeros((1, 1), F32)
    slot_row = jnp.zeros((1, nb), F32)
    group_lane = iota((1, 2 * nb), 1).astype(F32)
    group_type = jnp.zeros((1, 2 * nb), F32)
    for t in range(nt):
        slot_row = jnp.where(typ_row == t, GROUP * start + before[t : t + 1], slot_row)
        start = start + groups[t : t + 1]
        if t < nt - 1:
            group_type = group_type + jnp.where(start <= group_lane, 1.0, 0.0)
    slot_col = jnp.transpose(jnp.broadcast_to(slot_row, (nb, nb)))
    holds = onehot(jnp.concatenate([slot_col, slot_col], axis=1) == iota((nb, 2 * nb), 1).astype(F32))
    number = iota((8, nb), 1).astype(F32).astype(BF)
    idx_v[...] = jnp.zeros(idx_v.shape, jnp.int32)
    idx_v[0:1, :] = dot(number, holds)[0:1].astype(jnp.int32)
    idx_v[1:2, :] = jnp.concatenate([slot_row, slot_row], axis=1).astype(jnp.int32)
    idx_v[2:3, :] = group_type.astype(jnp.int32)


def kernel(
    n_r, n_c, rl, cl,
    r_ref, lib_ref, strap_ref, typ_ref, ids_ref, typ_s, idx_s,
    v_ref, res_ref,
    z_ref, w_ref, u_ref, t_ref, rb_ref, sorted_y, sorted_p,
    lib_w, inv_l, rs_l,
    own_idt, gat_idt, own_rho, gat_rho, own_tau, gat_tau,
    idsh, oh_all, acc, dacc, mat, mat_h, xmat,
    cedge_out, cedge_in, coarse_b,
    dots, own_sum, row_sum, own_col, col_sum,
    send_idt, recv_idt, send_rho, recv_rho, send_tau, recv_tau,
    send_halo, recv_halo, send_edge, recv_edge,
    send_rs, recv_rs, send_cs, recv_cs, load_sem,
):
    nt, nd, _ = lib_ref.shape
    nb = rl * cl
    sz = r_ref.shape[0]
    ng = acc.shape[0]
    slots = sorted_y.shape[0]
    me = lax.axis_index("row")
    mc = lax.axis_index("col")

    def row_peer(off):
        return {"row": lax.rem(me + off, n_r)}

    def col_peer(off):
        return {"col": lax.rem(mc + off, n_c)}

    barrier = pltpu.get_barrier_semaphore()

    def greet_row(off, carry):
        pl.semaphore_signal(barrier, inc=1, device_id=row_peer(off), device_id_type=MESH)
        return carry

    def greet_col(off, carry):
        pl.semaphore_signal(barrier, inc=1, device_id=col_peer(off), device_id_type=MESH)
        return carry

    load_copies = [pltpu.make_async_copy(r_ref.at[s], rb_ref.at[:, s], load_sem) for s in range(sz)]
    for copy in load_copies:
        copy.start()
    lax.fori_loop(1, n_r, greet_row, 0)
    lax.fori_loop(1, n_c, greet_col, 0)

    strap0 = strap_ref[0:1, :]
    strap1 = strap_ref[1:2, :]
    couple = 2.0 * strap0 + 2.0 * strap1
    nw = jnp.sum(strap0, axis=1, keepdims=True)
    ew = jnp.sum(strap1, axis=1, keepdims=True)
    eye = iota((nd, nd), 0) == iota((nd, nd), 1)
    id_row = flat_row(ids_ref, rl, cl)
    typ_row = flat_row(typ_ref, rl, cl)
    own_idt[0:1, :] = id_row
    own_idt[1:2, :] = typ_row

    sums = []
    for t in range(nt):
        lib = lib_ref[t]
        hi, lo = split2(lib)
        lib_w[t, 0:nd, 0:nd] = hi
        lib_w[t, nd : 2 * nd, 0:nd] = hi
        lib_w[t, 0:nd, nd : 2 * nd] = lo
        lib_w[t, nd : 2 * nd, nd : 2 * nd] = lo
        rows = jnp.sum(lib, axis=0, keepdims=True)
        sums.append(jnp.sum(rows, axis=1, keepdims=True))
        rs_l[t : t + 1, :] = rows
        inv_l[t : t + 1, :] = 1.0 / (jnp.sum(jnp.where(eye, lib, 0.0), axis=0, keepdims=True) + couple)

    def block_products(y, lib):
        both = dot(jnp.concatenate(split2(y), axis=1), lib)
        return both[:, :nd] + both[:, nd:]

    def smooth(load):
        def body(i, carry):
            for q in range(UNROLL):
                g = i * UNROLL + q
                kind = idx_s[2, g]
                lib = lib_w[kind]
                inv = inv_l[pl.ds(kind, 1), :]
                v = jnp.concatenate([load(idx_s[0, g * GROUP + j]) for j in range(GROUP)], axis=0)
                y = v * inv
                for sweep in range(2):
                    y = y + (v - block_products(y, lib) - couple * y) * inv
                sorted_y[pl.ds(g * GROUP, GROUP)] = y.reshape(GROUP, sz, nd)
                p = block_products(y, lib)
                sorted_p[pl.ds(g * GROUP, GROUP)] = p.reshape(GROUP, sz, nd)
            return carry

        lax.fori_loop(0, slots // (GROUP * UNROLL), body, 0)

    lane_b = iota((sz, nb), 1)

    def put_row(own, gathered, send, recv):
        def body(off, carry):
            pltpu.make_async_remote_copy(
                src_ref=own,
                dst_ref=gathered.at[me],
                send_sem=send,
                recv_sem=recv,
                device_id=row_peer(off),
                device_id_type=MESH,
            ).start()
            return carry

        lax.fori_loop(1, n_r, body, 0)
        gathered[pl.ds(me, 1)] = own[...][None]

    def wait_bytes(gathered, sem, count):
        part = gathered.at[pl.ds(0, count)]
        pltpu.make_async_copy(part, part, sem).wait()

    def regroup(r, rho):
        for c in range(cl):
            b = r * cl + c
            rho = jnp.where(lane_b == b, jnp.sum(rb_ref[b], axis=1, keepdims=True), rho)
        return rho

    pltpu.make_async_copy(rb_ref, rb_ref, load_sem).wait()
    own_rho[...] = lax.fori_loop(0, rl, regroup, jnp.zeros((sz, nb), F32))

    pl.semaphore_wait(barrier, n_r - 1 + n_c - 1)
    put_row(own_idt, gat_idt, send_idt, recv_idt)
    put_row(own_rho, gat_rho, send_rho, recv_rho)

    smooth(lambda b: rb_ref[b])

    north, south = me - 1, me + 1
    west, east = mc - 1, mc + 1
    has = (me > 0, me < n_r - 1, mc > 0, mc < n_c - 1)

    def halo_copies(rnd, field):
        where = ({"row": north}, {"row": south}, {"col": west}, {"col": east})
        inner_r, inner_c = pl.ds(1, rl), pl.ds(1, cl)
        sources = (field.at[1, inner_c], field.at[rl, inner_c], field.at[inner_r, 1], field.at[inner_r, cl])
        landing = (
            field.at[0, inner_c], field.at[rl + 1, inner_c], field.at[inner_r, 0], field.at[inner_r, cl + 1]
        )
        opposite = (1, 0, 3, 2)
        out = []
        for k in range(4):
            give = pltpu.make_async_remote_copy(
                src_ref=sources[k],
                dst_ref=landing[opposite[k]],
                send_sem=send_halo.at[rnd, k],
                recv_sem=recv_halo.at[rnd, k],
                device_id=where[k],
                device_id_type=MESH,
            )
            take = pltpu.make_async_copy(landing[k], landing[k], recv_halo.at[rnd, opposite[k]])
            out.append((has[k], give, take, landing[k]))
        return out

    def halo_start(rnd, field):
        for here, give, _, landing in halo_copies(rnd, field):

            @pl.when(here)
            def _():
                give.start()

            @pl.when(jnp.logical_not(here))
            def _():
                landing[...] = jnp.zeros(landing.shape, F32)

    def halo_wait(rnd, field):
        for here, give, take, _ in halo_copies(rnd, field):

            @pl.when(here)
            def _():
                take.wait()
                give.wait_send()

    def place_s(r, carry):
        for c in range(cl):
            z_ref[r + 1, c + 1] = sorted_y[idx_s[1, r * cl + c]]
        return carry

    lax.fori_loop(0, rl, place_s, 0)
    halo_start(0, z_ref)

    def lateral(field, r, c):
        f = field[r + 1, c + 1]
        fn = field[r, c + 1]
        fs = field[r + 2, c + 1]
        fw = field[r + 1, c]
        fe = field[r + 1, c + 2]
        return strap0 * (2.0 * f - fn - fs) + strap1 * (2.0 * f - fw - fe)

    halo_wait(0, z_ref)

    def image_s(r, tau):
        for c in range(cl):
            b = r * cl + c
            u = sorted_p[idx_s[1, b]] + lateral(z_ref, r, c)
            u_ref[b] = u
            tau = jnp.where(lane_b == b, jnp.sum(u, axis=1, keepdims=True), tau)
        return tau

    own_tau[...] = lax.fori_loop(0, rl, image_s, jnp.zeros((sz, nb), F32))
    put_row(own_tau, gat_tau, send_tau, recv_tau)

    wait_bytes(gat_idt, recv_idt, n_r - 1)
    ids = gat_idt[:, 0, :]
    typs = gat_idt[:, 1, :]
    lane = iota((n_r, nb), 1)
    none = jnp.full((1, nb), -1.0, F32)
    above = jnp.concatenate([none, ids[:-1]], axis=0)
    below = jnp.concatenate([ids[1:], none], axis=0)
    idsh[0] = ids
    idsh[1] = jnp.where(lane < cl, pltpu.roll(above, cl, 1), pltpu.roll(ids, cl, 1))
    idsh[2] = jnp.where(lane >= nb - cl, pltpu.roll(below, nb - cl, 1), pltpu.roll(ids, nb - cl, 1))
    idsh[3] = jnp.where(lax.rem(lane, cl) == 0, -1.0, pltpu.roll(ids, 1, 1))
    idsh[4] = jnp.where(lax.rem(lane, cl) == cl - 1, -1.0, pltpu.roll(ids, nb - 1, 1))
    centre = jnp.zeros((n_r, nb), F32)
    for t in range(nt):
        centre = jnp.where(typs == t, sums[t], centre)
    idsh[5] = centre + 2.0 * nw + 2.0 * ew

    acc[...] = jnp.zeros(acc.shape, F32)
    dacc[...] = jnp.zeros(dacc.shape, F32)
    agg = iota((ng, STEP * nb), 0).astype(F32)

    def assemble(k, carry):
        def several(j):
            return jnp.concatenate([idsh[j, pl.ds(STEP * k + i, 1), :] for i in range(STEP)], axis=1)

        here = agg == several(0)
        mask = onehot(here)
        oh_all[k] = mask
        other = jnp.concatenate([onehot(agg == several(2)), onehot(agg == several(4))], axis=0)
        acc[...] += dot(mask, other, LAST)
        weighted = jnp.where(here, several(5), 0.0)
        more = weighted[:, :nb]
        for i in range(1, STEP):
            more = more + weighted[:, i * nb : (i + 1) * nb]
        dacc[...] += more
        return carry

    lax.fori_loop(0, n_r // STEP, assemble, 0)
    big_eye = iota((ng, ng), 0) == iota((ng, ng), 1)
    cross = nw * acc[:, :ng] + ew * acc[:, ng:]
    total = jnp.sum(dacc[...], axis=1, keepdims=True)
    coarse = jnp.where(big_eye, total, 0.0) - cross - jnp.transpose(cross)
    on_diag = jnp.where(big_eye, coarse, 0.0)
    scale = lax.rsqrt(jnp.sum(on_diag, axis=0, keepdims=True))
    scaled = coarse * scale * lax.rsqrt(jnp.sum(on_diag, axis=1, keepdims=True))
    a_hi, a_mid, a_lo = split3(scaled)
    mat[0] = a_hi
    mat[1] = a_mid
    mat[2] = a_lo
    mat_h[:, 0:ng] = a_hi
    mat_h[:, ng : 2 * ng] = a_mid
    mat_h[:, 2 * ng : 3 * ng] = a_hi

    low = jnp.broadcast_to(0.0085 * ew / (nw + ew), (1, ng))
    mu = 2.0 / (1.0 + low)
    xmat[...] = jnp.where(big_eye, mu, 0.0) - (0.25 * mu * mu) * scaled
    low = 4.0 * low / ((1.0 + low) * (1.0 + low))

    def newton(i, low):
        mu = 2.0 / (1.0 + low)
        x = xmat[...]
        x_hi, x_lo = split2(x)
        t_hi, t_lo = split2(dot(mat_h[...], jnp.concatenate([x_hi, x_hi, x_lo], axis=0)))
        xt = dot(
            jnp.concatenate([x_hi, x_lo, x_hi], axis=1),
            jnp.concatenate([t_hi, t_hi, t_lo], axis=0),
        )
        xmat[...] = 2.0 * mu * x - (mu * mu) * xt
        return 4.0 * low / ((1.0 + low) * (1.0 + low))

    lax.fori_loop(0, NEWTON, newton, low)
    inv_hi, inv_lo = split2(xmat[...])

    def by_inverse(g):
        y = dot(jnp.concatenate(split2(g), axis=0), inv_hi)
        return y[:sz] + y[sz:] + dot(g.astype(BF), inv_lo)

    def by_matrix(c):
        c_hi, c_mid, c_lo = split3(c)
        y = dot(jnp.concatenate([c_hi, c_mid, c_lo], axis=0), mat[0])
        x = dot(jnp.concatenate([c_hi, c_mid], axis=0), mat[1])
        return (y[2 * sz :] + x[sz:] + dot(c_hi, mat[2])) + (y[sz : 2 * sz] + x[:sz]) + y[:sz]

    def solve(g):
        g = g * scale
        c = by_inverse(g)
        for _ in range(REFINE):
            c = c + by_inverse(g - by_matrix(c))
        return c * scale

    def aggregate(gathered):
        def body(k, total):
            x = jnp.concatenate([gathered[STEP * k + i] for i in range(STEP)], axis=1)
            return total + rows_dot(x, oh_all[k], LAST)

        return lax.fori_loop(0, n_r // STEP, body, jnp.zeros((sz, ng), F32))

    wait_bytes(gat_rho, recv_rho, n_r - 1)
    sums_r = aggregate(gat_rho)
    c = solve(sums_r)

    pick = iota((nb, nb), 0)
    slot = iota((nb, nb), 1)
    first = dot(ids.astype(BF), onehot(pick == slot * cl))
    final = dot(ids.astype(BF), onehot(pick == slot * cl + cl - 1))
    agg_lane = iota((n_r, ng), 1).astype(F32)
    oh_first = jnp.concatenate([onehot(first[:, j : j + 1] == agg_lane) for j in range(rl)], axis=0)
    oh_final = jnp.concatenate([onehot(final[:, j : j + 1] == agg_lane) for j in range(rl)], axis=0)
    cedge_out[0] = rows_dot(c, oh_first, LAST)
    cedge_out[1] = rows_dot(c, oh_final, LAST)

    def edge_copies():
        out = []
        for k, to in ((0, west), (1, east)):
            give = pltpu.make_async_remote_copy(
                src_ref=cedge_out.at[k],
                dst_ref=cedge_in.at[1 - k],
                send_sem=send_edge.at[k],
                recv_sem=recv_edge.at[k],
                device_id={"col": to},
                device_id_type=MESH,
            )
            take = pltpu.make_async_copy(cedge_in.at[k], cedge_in.at[k], recv_edge.at[1 - k])
            out.append((has[2 + k], give, take, cedge_in.at[k]))
        return out

    for here, give, _, landing in edge_copies():

        @pl.when(here)
        def _():
            give.start()

        @pl.when(jnp.logical_not(here))
        def _():
            landing[...] = jnp.zeros(landing.shape, F32)

    tall = iota((ng, nb), 0).astype(F32)

    def local_onehot(j):
        return onehot(tall == idsh[j, pl.ds(me, 1), :])

    oh_own = local_onehot(0)
    oh_we = local_onehot(3) + local_onehot(4)
    oh_own_ns = jnp.concatenate([oh_own, local_onehot(1) + local_onehot(2)], axis=1)
    c_own_ns = rows_dot(c, oh_own_ns, PLAIN)
    coarse_b[0] = c_own_ns[:, 0:nb]
    coarse_b[1] = c_own_ns[:, nb:]
    coarse_b[2] = rows_dot(c, oh_we, PLAIN)
    wait_bytes(gat_tau, recv_tau, n_r - 1)
    sums_u = aggregate(gat_tau) + sums_r

    for here, give, take, _ in edge_copies():

        @pl.when(here)
        def _():
            take.wait()
            give.wait_send()

    block = iota((ng, nb), 1)
    spot = iota((ng, nb), 0) == (block // cl) * n_r + me
    at_west = onehot(jnp.logical_and(lax.rem(block, cl) == 0, spot))
    at_east = onehot(jnp.logical_and(lax.rem(block, cl) == cl - 1, spot))
    from_west = cedge_in[0]
    from_east = cedge_in[1]
    at_sides = jnp.concatenate([at_west, at_east], axis=1)
    coarse_b[2] = (
        coarse_b[2] + rows_dot(from_west, at_sides, PLAIN)[:, :nb] + rows_dot(from_east, at_sides, PLAIN)[:, nb:]
    )
    over = rows_dot(from_west, oh_first, PLAIN) + rows_dot(from_east, oh_final, PLAIN)
    d = solve(sums_u - ew * over)
    coarse_b[3] = rows_dot(d, oh_own_ns, PLAIN)[:, :nb]

    def turned(j, r):
        return pltpu.roll(coarse_b[j], lax.rem(nb - r * cl, nb), 1)

    def apply_c(r, carry):
        own, ns, we = turned(0, r), turned(1, r), turned(2, r)
        for c in range(cl):
            b = r * cl + c
            rs = rs_l[pl.ds(typ_s[r, c], 1), :] + couple
            mid = own[:, c : c + 1]
            z_ref[r + 1, c + 1] += jnp.broadcast_to(mid, (sz, nd))
            u_ref[b] += mid * rs - ns[:, c : c + 1] * strap0 - we[:, c : c + 1] * strap1
        return carry

    lax.fori_loop(0, rl, apply_c, 0)
    smooth(lambda b: u_ref[b])

    def place_w(r, carry):
        extra = turned(3, r)
        for c in range(cl):
            w_ref[r + 1, c + 1] = sorted_y[idx_s[1, r * cl + c]] + extra[:, c : c + 1]
        return carry

    lax.fori_loop(0, rl, place_w, 0)
    halo_start(1, w_ref)
    halo_wait(1, w_ref)

    def finish(row, parts):
        extra = turned(3, row)
        for c in range(cl):
            b = row * cl + c
            rs = rs_l[pl.ds(typ_s[row, c], 1), :]
            t = sorted_p[idx_s[1, b]] + extra[:, c : c + 1] * rs + lateral(w_ref, row, c)
            t_ref[b] = t
            r, z, u, w = rb_ref[b], z_ref[row + 1, c + 1], u_ref[b], w_ref[row + 1, c + 1]
            pairs = ((r, z), (z, u), (r, w), (u, w), (z, t), (w, t))
            parts = tuple(p + x * y for p, (x, y) in zip(parts, pairs))
        return parts

    parts = lax.fori_loop(0, rl, finish, tuple(jnp.zeros((sz, nd), F32) for _ in range(6)))

    lane_s = iota((sz, nd), 1)
    row_s = iota((sz, nd), 0)
    packed = jnp.zeros((sz, nd), F32)
    for k in range(6):
        value = jnp.sum(parts[k], axis=1, keepdims=True)
        packed = packed + jnp.where(lane_s == row_s * 8 + k, value, 0.0)
    own_sum[...] = jnp.sum(packed, axis=0, keepdims=True)
    put_row(own_sum, row_sum, send_rs, recv_rs)
    wait_bytes(row_sum, recv_rs, n_r - 1)
    own_col[...] = jnp.sum(row_sum[...], axis=0)

    def put_col(off, carry):
        pltpu.make_async_remote_copy(
            src_ref=own_col,
            dst_ref=col_sum.at[mc],
            send_sem=send_cs,
            recv_sem=recv_cs,
            device_id=col_peer(off),
            device_id_type=MESH,
        ).start()
        return carry

    lax.fori_loop(1, n_c, put_col, 0)
    col_sum[pl.ds(mc, 1)] = own_col[...][None]
    wait_bytes(col_sum, recv_cs, n_c - 1)
    every = jnp.broadcast_to(jnp.sum(col_sum[...], axis=0), (sz, nd))

    def unpack(k):
        return jnp.sum(jnp.where(lane_s == row_s * 8 + k, every, 0.0), axis=1, keepdims=True)

    rz, zu, rw, uw, zt, wt = [unpack(k) for k in range(6)]
    step0 = rz / zu
    fresh = rz - step0 * (rw + zu) + step0 * step0 * uw
    blend1 = 1.0 + fresh / rz
    curv = blend1 * blend1 * zu - blend1 * step0 * (zt + uw) + step0 * step0 * wt
    step1 = fresh / curv
    on_first = jnp.broadcast_to(step0 + step1 * blend1, (sz, nd))
    on_second = jnp.broadcast_to(step0 * step1, (sz, nd))

    def output(r, carry):
        for c in range(cl):
            b = r * cl + c
            v_ref[b] = on_first * z_ref[r + 1, c + 1] - on_second * w_ref[r + 1, c + 1]
            res_ref[b] = rb_ref[b] - on_first * u_ref[b] + on_second * t_ref[b]
        return carry

    lax.fori_loop(0, rl, output, 0)

    wait_bytes(gat_idt, send_idt, n_r - 1)
    wait_bytes(gat_rho, send_rho, n_r - 1)
    wait_bytes(gat_tau, send_tau, n_r - 1)
    wait_bytes(row_sum, send_rs, n_r - 1)
    wait_bytes(col_sum, send_cs, n_c - 1)


def on_device(n_r, n_c, load_currents, block_library, strap_conductance, block_types, aggregate_map):
    sz, rl, cl, nd = load_currents.shape
    nt = block_library.shape[0]
    nb = rl * cl
    ng = n_r * rl // AGR * (cl // AGC)
    per_turn = GROUP * UNROLL
    slots = -(-(nb + nt * (GROUP - 1)) // per_turn) * per_turn
    vmem = pl.BlockSpec(memory_space=pltpu.VMEM)
    smem = pl.BlockSpec(memory_space=pltpu.SMEM)
    padded = pltpu.VMEM((rl + 2, cl + 2, sz, nd), F32)
    field = pltpu.VMEM((nb, sz, nd), F32)
    ordered = pltpu.VMEM((slots, sz, nd), F32)
    shape = jax.ShapeDtypeStruct((nb, sz, nd), F32)
    dma = pltpu.SemaphoreType.DMA
    order = pl.pallas_call(
        functools.partial(order_kernel, nt),
        out_shape=jax.ShapeDtypeStruct((8, 2 * nb), jnp.int32),
        in_specs=[vmem],
        out_specs=vmem,
    )(block_types)
    v, res = pl.pallas_call(
        functools.partial(kernel, n_r, n_c, rl, cl),
        out_shape=(shape, shape),
        in_specs=[pl.BlockSpec(memory_space=pl.ANY)] + [vmem] * 4 + [smem, smem],
        out_specs=(vmem, vmem),
        scratch_shapes=[
            padded, padded, field, field, field, ordered, ordered,
            pltpu.VMEM((nt, 2 * nd, 2 * nd), BF), pltpu.VMEM((nt, nd), F32), pltpu.VMEM((nt, nd), F32),
            pltpu.VMEM((2, nb), F32), pltpu.VMEM((n_r, 2, nb), F32),
            pltpu.VMEM((sz, nb), F32), pltpu.VMEM((n_r, sz, nb), F32),
            pltpu.VMEM((sz, nb), F32), pltpu.VMEM((n_r, sz, nb), F32),
            pltpu.VMEM((6, n_r, nb), F32), pltpu.VMEM((n_r // STEP, ng, STEP * nb), BF),
            pltpu.VMEM((ng, 2 * ng), F32), pltpu.VMEM((ng, nb), F32),
            pltpu.VMEM((3, ng, ng), BF), pltpu.VMEM((ng, 3 * ng), BF), pltpu.VMEM((ng, ng), F32),
            pltpu.VMEM((2, sz, ng), F32), pltpu.VMEM((2, sz, ng), F32), pltpu.VMEM((4, sz, nb), F32),
            pltpu.VMEM((6, sz, nd), F32), pltpu.VMEM((1, nd), F32), pltpu.VMEM((n_r, 1, nd), F32),
            pltpu.VMEM((1, nd), F32), pltpu.VMEM((n_c, 1, nd), F32),
            dma, dma, dma, dma, dma, dma,
            dma((2, 4)), dma((2, 4)), dma((2,)), dma((2,)),
            dma, dma, dma, dma, dma,
        ],
        compiler_params=pltpu.CompilerParams(
            collective_id=0, has_side_effects=True, vmem_limit_bytes=56 * 1024 * 1024
        ),
    )(
        load_currents.reshape(sz, nb, nd), block_library, strap_conductance,
        block_types, aggregate_map, block_types, order,
    )
    back = lambda x: jnp.swapaxes(x, 0, 1).reshape(load_currents.shape)
    return back(v), back(res)


def solution(mesh):
    placed = (P(None, "row", "col", None), P(), P(), P("row", "col"), P("row", "col"))
    return jax.shard_map(
        functools.partial(on_device, mesh.shape["row"], mesh.shape["col"]),
        mesh=mesh,
        in_specs=placed,
        out_specs=(P(None, "row", "col", None), P(None, "row", "col", None)),
        check_vma=False,
    )
```

time: 70.5 us -> 73.2 us (1.038)
  Pallas kernels: 66.3 us -> 68.4 us
    pallas_call x1 -> x2, Pallas kernels: 66.3 us -> 68.4 us  [the longest x1 66.6 us: on_device(): pl.pallas_call(functools.partial(kernel, n_r, n_c, rl, cl), out_shape=(sh...]
where the time goes in v2:
time: 73.2 us; the launch traced here: 73 us
  Pallas kernels  68.4 us (93%)
  local copies, waits for them, and re-layouts  3.92 us (5%)
    pallas_call x1, Pallas kernels, on_device(): pl.pallas_call(functools.partial(kernel, n_r, n_c, rl, cl), out_shape=(sh...  66.6 us
    unnamed x4, local copies, waits for them, and re-layouts  3.92 us
    pallas_call x1, Pallas kernels, on_device(): pl.pallas_call(functools.partial(order_kernel, nt), out_shape=jax.ShapeDt...  1.8 us

profile of v2, /device:TPU:1, one launch (start us, length us, event | category | flops | bytes accessed | tf_op | source)
XLA Modules:
  0.0 73.0 jit_solution(6407181549053513924)
XLA Ops:
  0.6 1.8 %shard_map.68.idx_s = s32[8,256]{1,0:T(8,128)} custom-call(s32[8,16]{1,0:T(8,128)} %typ_s.1), custom_call_target="tpu_custom_call" | custom-call | tf_op jit(solution)/shard_map/pallas_call | solution.py:577
  2.4 66.6 %shard_map.69 = (f32[128,16,128]{2,1,0:T(8,128)}, f32[128,16,128]{2,1,0:T(8,128)}) custom-call(f32[16,128,128]{2,1,0:T(8,128)} %bitcast.7, f32[8,128,128]{2,1,0:T(8,128)} %lib_ref.1, f32[2,128]{1,0:T(2,128)} %strap_ref.1, s32[8,16]{1,0:T(8,128)} %typ_s.1, s32[8,16]{1,0:T(8,128)} %ids_ref.1, s32[8,16]{1,0:T(8,128)} %typ_s.1, s32[8,256]{1,0:T(8,128)} %shard_map.68.idx_s), custom_call_target="tpu_custom_call" | custom-call | tf_op jit(solution)/shard_map/pallas_call | solution.py:583
  69.1 0.0 copy-start
  69.1 2.6 %copy.7 = f32[16,8,16,128]{3,2,1,0:T(8,128)} copy(f32[16,8,16,128]{3,0,2,1:T(8,128)} %bitcast.9) | data formatting | bytes 2097152
  71.7 0.0 copy-done
  71.7 1.3 %copy.8 = f32[16,8,16,128]{3,2,1,0:T(8,128)} copy(f32[16,8,16,128]{3,0,2,1:T(8,128)S(1)} %bitcast.8) | data formatting | bytes 2097152
Async XLA Ops:
  69.1 2.6 %copy-start = (f32[128,16,128]{2,1,0:T(8,128)S(1)}, f32[128,16,128]{2,1,0:T(8,128)}, u32[]{:S(2)}) copy-start(f32[128,16,128]{2,1,0:T(8,128)} %get-tuple-element.5) | copy-start | bytes 3145732
